TPU v7x, 32 devices: a whole 2x2x4 slice. The times are simulated.
32 devices in a mesh: slab: 4 (over x, core), panel: 8 (over z, y).
Axes of the slice: x: 2, y: 2, z: 4, core: 2. Of those that a mesh axis runs over, the one named last changes fastest.
Arguments:
- ranges: float32 [4, 4, 1024, 1024], P('slab', None, 'panel'), may hold values from -1.5 to 1.5
- pattern: int32 [4, 4, 16, 16], P('slab'), may hold values 0 or 1
Outputs:
- combined: float32 [4, 4, 1024, 1024], P('slab', None, 'panel')
All inputs are finite; a program needn't handle non-finite values. No bound on the sum of `pattern` on one device may be relied on, other than what follows from the above.
Results may differ from a plain program's by a relative error of at most 0.01.
Values may be sent and summed in bfloat16 or wider, within the bound.
A program may use at most 64 MiB of HBM per device.

v0:
```python
import jax
import jax.numpy as jnp
from jax import lax
from jax.sharding import PartitionSpec as P

M = 1024
BLK = 64
LEVELS = 2


def partner_2(block, axis, distance):
    count = lax.axis_size(axis)
    route = []
    for low in range(count):
        high = low | 1 << distance
        if high != low and high < count:
            route += [(low, high), (high, low)]
    return lax.ppermute(block, axis, route)


def to_half(values):
    return values.astype(jnp.bfloat16)


def star(head, tail, tree_level, row_start):
    head_top, head_up, head_down, head_bottom = (head[0], head[1], head[2], head[3])
    tail_top, tail_up, tail_down, tail_bottom = (tail[0], tail[1], tail[2], tail[3])
    local_rows = head.shape[1]
    col_side = lax.axis_index("slab") >> tree_level & 1
    col_start = col_side * (M // 2)

    def cut_cols(values):
        return lax.dynamic_slice_in_dim(to_half(values), col_start, M // 2, 1)

    right_bottom, right_up, right_down = (
        lax.all_gather(cut_cols(head_bottom), "panel", axis=0, tiled=True),
        lax.all_gather(cut_cols(tail_up), "panel", axis=0, tiled=True),
        lax.all_gather(cut_cols(head_down), "panel", axis=0, tiled=True),
    )

    def spread(values):
        return lax.all_gather(cut_cols(values), "panel", axis=0, tiled=True)

    def multiply(left, right):
        half_cols = jnp.dot(to_half(left), right, preferred_element_type=jnp.float32)
        other_cols = partner_2(half_cols, "slab", tree_level)
        return jnp.where(
            col_side == 0,
            jnp.concatenate([half_cols, other_cols], 1),
            jnp.concatenate([other_cols, half_cols], 1),
        )

    col_ids = col_start + jnp.arange(M // 2, dtype=jnp.int32)
    all_ids = jnp.arange(M, dtype=jnp.int32)
    eye_right = (all_ids[:, None] == col_ids[None, :]).astype(jnp.float32)
    row_ids = row_start + jnp.arange(local_rows, dtype=jnp.int32)
    eye_rows = (row_ids[:, None] == all_ids[None, :]).astype(jnp.float32)
    loop_term = multiply(tail_top, right_bottom)
    loop_kept = lax.optimization_barrier(to_half(loop_term)).astype(jnp.float32)
    right_loop = spread(loop_term)
    right_defect = to_half(eye_right - right_loop.astype(jnp.float32))
    right_guess = to_half(eye_right + right_loop.astype(jnp.float32))
    guess = eye_rows + loop_kept
    guess = 2.0 * guess - multiply(multiply(guess, right_defect), right_guess)
    right_inverse = spread(guess)
    lifted = multiply(head_up, right_inverse)
    joint_up = multiply(lifted, right_up)
    bounce = multiply(tail_top, right_down)
    right_bounce = spread(bounce)
    joint_top = head_top + multiply(lifted, right_bounce)
    reach = multiply(tail_down, right_bottom)
    through = multiply(reach, right_inverse)
    joint_down = multiply(tail_down, right_down) + multiply(through, right_bounce)
    joint_bottom = (
        tail_bottom + multiply(reach, right_up) + multiply(multiply(through, right_loop), right_up)
    )
    return jnp.stack([joint_top, joint_up, joint_down, joint_bottom])


def body(ranges, pattern):
    group_blocks = ranges[0]
    local_rows = group_blocks.shape[1]
    block_count = pattern.shape[2]
    row_start = lax.axis_index("panel") * local_rows
    row_ids = row_start + jnp.arange(local_rows, dtype=jnp.int32)
    col_ids = jnp.arange(M, dtype=jnp.int32)
    block_ids = jnp.arange(block_count, dtype=jnp.int32)
    row_pick = (row_ids[:, None] // BLK == block_ids[None, :]).astype(jnp.float32)
    col_pick = (block_ids[:, None] == col_ids[None, :] // BLK).astype(jnp.float32)
    block_mask = jnp.einsum("mi,gij,jc->gmc", row_pick, pattern[0].astype(jnp.float32), col_pick)
    merged = group_blocks * block_mask
    for tree_level in range(LEVELS):
        partner = partner_2(merged, "slab", tree_level)
        is_lower = lax.axis_index("slab") >> tree_level & 1 == 0
        head_blocks = jnp.where(is_lower, merged, partner)
        tail_blocks = jnp.where(is_lower, partner, merged)
        merged = star(head_blocks, tail_blocks, tree_level, row_start)
    return merged[None]


def solution(mesh):
    return jax.shard_map(
        body,
        mesh=mesh,
        in_specs=(P("slab", None, "panel", None), P("slab", None, None, None)),
        out_specs=P("slab", None, "panel", None),
        check_vma=False,
    )
```

profile of v0, /device:TPU:0, one launch (start us, length us, event | category | flops | bytes accessed | tf_op | source)
XLA Modules:
  0.0 616.8 jit_solution(5166546670370426008)
XLA Ops:
  6.6 2.3 bitcast_multiply_fusion
  9.4 3.9 collective-permute-done
  13.3 4.4 fusion.131
  19.5 43.0 %all-gather.31.cloned.1.call-done = bf16[1,1024,512]{2,1,0:T(8,128)(2,1)} async-done(((bf16[1,128,512]{2,1,0:T(8,128)(2,1)}), bf16[1,1024,512]{2,1,0:T(8,128)(2,1)}) %all-gather.31.cloned.1.call-update) | async-done | bytes 1048592 | tf_op jit(solution)/shard_map/all_gather | solution.py:36
  67.8 37.5 %all-gather.19.cloned.1.call-done = bf16[1024,512]{1,0:T(8,128)(2,1)} async-done(((bf16[128,512]{1,0:T(8,128)(2,1)}), bf16[1024,512]{1,0:T(8,128)(2,1)}) %all-gather.19.cloned.1.call-update) | async-done | bytes 1048592 | tf_op jit(solution)/shard_map/all_gather | solution.py:42
  111.7 34.8 %all-gather.33.cloned.1.call-done = bf16[1,1024,512]{2,1,0:T(8,128)(2,1)} async-done(((bf16[1,128,512]{2,1,0:T(8,128)(2,1)}), bf16[1,1024,512]{2,1,0:T(8,128)(2,1)}) %all-gather.33.cloned.1.call-update) | async-done | bytes 1048592 | tf_op jit(solution)/shard_map/all_gather | solution.py:38
  151.7 35.8 %all-gather.35.cloned.1.call-done = bf16[1,1024,512]{2,1,0:T(8,128)(2,1)} async-done(((bf16[1,128,512]{2,1,0:T(8,128)(2,1)}), bf16[1,1024,512]{2,1,0:T(8,128)(2,1)}) %all-gather.35.cloned.1.call-update) | async-done | bytes 1048592 | tf_op jit(solution)/shard_map/all_gather | solution.py:37
  189.2 39.4 %all-gather.21.cloned.1.call-done = bf16[1024,512]{1,0:T(8,128)(2,1)} async-done(((bf16[128,512]{1,0:T(8,128)(2,1)}), bf16[1024,512]{1,0:T(8,128)(2,1)}) %all-gather.21.cloned.1.call-update) | async-done | bytes 1048592 | tf_op jit(solution)/shard_map/all_gather | solution.py:42
  232.6 37.0 %all-gather.23.cloned.1.call-done = bf16[1024,512]{1,0:T(8,128)(2,1)} async-done(((bf16[128,512]{1,0:T(8,128)(2,1)}), bf16[1024,512]{1,0:T(8,128)(2,1)}) %all-gather.23.cloned.1.call-update) | async-done | bytes 1048592 | tf_op jit(solution)/shard_map/all_gather | solution.py:42
  279.7 46.5 %collective-permute-done.15 = f32[4,128,1024]{2,1,0:T(8,128)} collective-permute-done((f32[4,128,1024]{2,1,0:T(8,128)}, f32[4,128,1024]{2,1,0:T(8,128)}, u32[]{:S(2)}, u32[]{:S(2)}) %collective-permute-start.15) | collective-permute-done | bytes 2097184 | tf_op jit(solution)/shard_map/ppermute | solution.py:18
  326.2 4.4 fusion.129
  332.4 39.1 %all-gather.37.cloned.1.call-done = bf16[1,1024,512]{2,1,0:T(8,128)(2,1)} async-done(((bf16[1,128,512]{2,1,0:T(8,128)(2,1)}), bf16[1,1024,512]{2,1,0:T(8,128)(2,1)}) %all-gather.37.cloned.1.call-update) | async-done | bytes 1048592 | tf_op jit(solution)/shard_map/all_gather | solution.py:36
  374.6 3.5 collective-permute-done.16
  380.5 37.6 %all-gather.25.cloned.1.call-done = bf16[1024,512]{1,0:T(8,128)(2,1)} async-done(((bf16[128,512]{1,0:T(8,128)(2,1)}), bf16[1024,512]{1,0:T(8,128)(2,1)}) %all-gather.25.cloned.1.call-update) | async-done | bytes 1048592 | tf_op jit(solution)/shard_map/all_gather | solution.py:42
  421.4 3.5 collective-permute-done.17
  427.2 4.7 collective-permute-done.18
  433.0 26.2 %all-gather.39.cloned.1.call-done = bf16[1,1024,512]{2,1,0:T(8,128)(2,1)} async-done(((bf16[1,128,512]{2,1,0:T(8,128)(2,1)}), bf16[1,1024,512]{2,1,0:T(8,128)(2,1)}) %all-gather.39.cloned.1.call-update) | async-done | bytes 1048592 | tf_op jit(solution)/shard_map/all_gather | solution.py:38
  462.3 3.5 collective-permute-done.20
  469.4 30.8 %all-gather.41.cloned.1.call-done = bf16[1,1024,512]{2,1,0:T(8,128)(2,1)} async-done(((bf16[1,128,512]{2,1,0:T(8,128)(2,1)}), bf16[1,1024,512]{2,1,0:T(8,128)(2,1)}) %all-gather.41.cloned.1.call-update) | async-done | bytes 1048592 | tf_op jit(solution)/shard_map/all_gather | solution.py:37
  503.2 38.1 %all-gather.27.cloned.1.call-done = bf16[1024,512]{1,0:T(8,128)(2,1)} async-done(((bf16[128,512]{1,0:T(8,128)(2,1)}), bf16[1024,512]{1,0:T(8,128)(2,1)}) %all-gather.27.cloned.1.call-update) | async-done | bytes 1048592 | tf_op jit(solution)/shard_map/all_gather | solution.py:42
  546.5 3.0 collective-permute-done.25
  550.3 32.0 %all-gather.29.cloned.1.call-done = bf16[1024,512]{1,0:T(8,128)(2,1)} async-done(((bf16[128,512]{1,0:T(8,128)(2,1)}), bf16[1024,512]{1,0:T(8,128)(2,1)}) %all-gather.29.cloned.1.call-update) | async-done | bytes 1048592 | tf_op jit(solution)/shard_map/all_gather | solution.py:42
  588.6 10.2 %collective-permute-done.22 = f32[128,512]{1,0:T(8,128)S(1)} collective-permute-done((f32[128,512]{1,0:T(8,128)S(1)}, f32[128,512]{1,0:T(8,128)S(1)}, u32[]{:S(2)}, u32[]{:S(2)}) %collective-permute-start.22) | collective-permute-done | bytes 262176 | tf_op jit(solution)/shard_map/ppermute | solution.py:18
  600.3 4.1 collective-permute-done.26
  (172 shorter events, 77.3 us)
Async XLA Ops:
  6.5 56.0 %all-gather.31.cloned.1.call-start = ((), (), s32[]{:S(2)}) async-start(), calls=%async_computation.6 | async-start | bytes 1179648 | tf_op jit(solution)/shard_map/all_gather | solution.py:36
  19.5 85.9 %all-gather.19.cloned.1.call-start = ((), (), s32[]{:S(2)}) async-start(), calls=%async_computation | async-start | bytes 1179648 | tf_op jit(solution)/shard_map/all_gather | solution.py:42
  66.2 80.3 %all-gather.33.cloned.1.call-start = ((), (), s32[]{:S(2)}) async-start(), calls=%async_computation.7 | async-start | bytes 1179648 | tf_op jit(solution)/shard_map/all_gather | solution.py:38
  67.0 120.6 %all-gather.35.cloned.1.call-start = ((), (), s32[]{:S(2)}) async-start(), calls=%async_computation.8 | async-start | bytes 1179648 | tf_op jit(solution)/shard_map/all_gather | solution.py:37
  67.8 160.8 %all-gather.21.cloned.1.call-start = ((), (), s32[]{:S(2)}) async-start(), calls=%async_computation.1 | async-start | bytes 1179648 | tf_op jit(solution)/shard_map/all_gather | solution.py:42
  111.7 157.9 %all-gather.23.cloned.1.call-start = ((), (), s32[]{:S(2)}) async-start(), calls=%async_computation.2 | async-start | bytes 1179648 | tf_op jit(solution)/shard_map/all_gather | solution.py:42
  150.4 221.2 %all-gather.37.cloned.1.call-start = ((), (), s32[]{:S(2)}) async-start(), calls=%async_computation.9 | async-start | bytes 1179648 | tf_op jit(solution)/shard_map/all_gather | solution.py:36
  150.7 36.8 %collective-permute-start.9 = (bf16[128,512]{1,0:T(8,128)(2,1)S(1)}, bf16[128,512]{1,0:T(8,128)(2,1)S(1)}, u32[]{:S(2)}, u32[]{:S(2)}) collective-permute-start(bf16[128,512]{1,0:T(8,128)(2,1)S(1)} %fusion.36), channel_id=1, source_target_pairs={{0,8},{8,0},{16,24},{24,16},{1,9},{9,1},{17,25},{25,17},{2,10},{10... | collective-permute-start | bytes 393224 | tf_op jit(solution)/shard_map/ppermute | solution.py:18
  151.3 122.5 %collective-permute-start.8 = (f32[128,512]{1,0:T(8,128)S(1)}, f32[128,512]{1,0:T(8,128)S(1)}, u32[]{:S(2)}, u32[]{:S(2)}) collective-permute-start(f32[128,512]{1,0:T(8,128)S(1)} %fusion.32), channel_id=1, source_target_pairs={{0,8},{8,0},{16,24},{24,16},{1,9},{9,1},{17,25},{25,17},{2,10},{10... | collective-permute-start | bytes 786440 | tf_op jit(solution)/shard_map/ppermute | solution.py:18
  189.1 86.4 %collective-permute-start.12 = (f32[128,512]{1,0:T(8,128)S(1)}, f32[128,512]{1,0:T(8,128)S(1)}, u32[]{:S(2)}, u32[]{:S(2)}) collective-permute-start(f32[128,512]{1,0:T(8,128)S(1)} %fusion.28), channel_id=1, source_target_pairs={{0,8},{8,0},{16,24},{24,16},{1,9},{9,1},{17,25},{25,17},{2,10},{10... | collective-permute-start | bytes 786440 | tf_op jit(solution)/shard_map/ppermute | solution.py:18
  231.6 38.0 %collective-permute-start.4 = (bf16[128,512]{1,0:T(8,128)(2,1)S(1)}, bf16[128,512]{1,0:T(8,128)(2,1)S(1)}, u32[]{:S(2)}, u32[]{:S(2)}) collective-permute-start(bf16[128,512]{1,0:T(8,128)(2,1)S(1)} %fusion.83), channel_id=1, source_target_pairs={{0,8},{8,0},{16,24},{24,16},{1,9},{9,1},{17,25},{25,17},{2,10},{10... | collective-permute-start | bytes 393224 | tf_op jit(solution)/shard_map/ppermute | solution.py:18
  232.5 40.0 %collective-permute-start.13 = (bf16[128,512]{1,0:T(8,128)(2,1)S(1)}, bf16[128,512]{1,0:T(8,128)(2,1)S(1)}, u32[]{:S(2)}, u32[]{:S(2)}) collective-permute-start(bf16[128,512]{1,0:T(8,128)(2,1)S(1)} %fusion.119), channel_id=1, source_target_pairs={{0,8},{8,0},{16,24},{24,16},{1,9},{9,1},{17,25},{25,17},{2,10},{10... | collective-permute-start | bytes 393224 | tf_op jit(solution)/shard_map/ppermute | solution.py:18
  278.3 48.0 %collective-permute-start.15 = (f32[4,128,1024]{2,1,0:T(8,128)}, f32[4,128,1024]{2,1,0:T(8,128)}, u32[]{:S(2)}, u32[]{:S(2)}) collective-permute-start(f32[4,128,1024]{2,1,0:T(8,128)} %pad_maximum_fusion), channel_id=1, source_target_pairs={{0,16},{16,0},{8,24},{24,8},{1,17},{17,1},{9,25},{25,9},{2,18},{18... | collective-permute-start | bytes 6291464 | tf_op jit(solution)/shard_map/ppermute | solution.py:18
  332.4 85.6 %all-gather.25.cloned.1.call-start = ((), (), s32[]{:S(2)}) async-start(), calls=%async_computation.3 | async-start | bytes 1179648 | tf_op jit(solution)/shard_map/all_gather | solution.py:42
  378.9 80.3 %all-gather.39.cloned.1.call-start = ((), (), s32[]{:S(2)}) async-start(), calls=%async_computation.10 | async-start | bytes 1179648 | tf_op jit(solution)/shard_map/all_gather | solution.py:38
  379.6 120.5 %all-gather.41.cloned.1.call-start = ((), (), s32[]{:S(2)}) async-start(), calls=%async_computation.11 | async-start | bytes 1179648 | tf_op jit(solution)/shard_map/all_gather | solution.py:37
  380.4 160.9 %all-gather.27.cloned.1.call-start = ((), (), s32[]{:S(2)}) async-start(), calls=%async_computation.4 | async-start | bytes 1179648 | tf_op jit(solution)/shard_map/all_gather | solution.py:42
  432.7 149.6 %all-gather.29.cloned.1.call-start = ((), (), s32[]{:S(2)}) async-start(), calls=%async_computation.5 | async-start | bytes 1179648 | tf_op jit(solution)/shard_map/all_gather | solution.py:42
  466.9 33.2 %collective-permute-start.24 = (bf16[128,512]{1,0:T(8,128)(2,1)S(1)}, bf16[128,512]{1,0:T(8,128)(2,1)S(1)}, u32[]{:S(2)}, u32[]{:S(2)}) collective-permute-start(bf16[128,512]{1,0:T(8,128)(2,1)S(1)} %fusion.22), channel_id=1, source_target_pairs={{0,16},{16,0},{8,24},{24,8},{1,17},{17,1},{9,25},{25,9},{2,18},{18... | collective-permute-start | bytes 393224 | tf_op jit(solution)/shard_map/ppermute | solution.py:18
  468.8 131.6 %collective-permute-start.23 = (f32[128,512]{1,0:T(8,128)S(1)}, f32[128,512]{1,0:T(8,128)S(1)}, u32[]{:S(2)}, u32[]{:S(2)}) collective-permute-start(f32[128,512]{1,0:T(8,128)S(1)} %fusion.18), channel_id=1, source_target_pairs={{0,16},{16,0},{8,24},{24,8},{1,17},{17,1},{9,25},{25,9},{2,18},{18... | collective-permute-start | bytes 786440 | tf_op jit(solution)/shard_map/ppermute | solution.py:18
  501.7 104.1 %collective-permute-start.27 = (f32[128,512]{1,0:T(8,128)S(1)}, f32[128,512]{1,0:T(8,128)S(1)}, u32[]{:S(2)}, u32[]{:S(2)}) collective-permute-start(f32[128,512]{1,0:T(8,128)S(1)} %fusion.14), channel_id=1, source_target_pairs={{0,16},{16,0},{8,24},{24,8},{1,17},{17,1},{9,25},{25,9},{2,18},{18... | collective-permute-start | bytes 786440 | tf_op jit(solution)/shard_map/ppermute | solution.py:18
  545.8 36.5 %collective-permute-start.19 = (bf16[128,512]{1,0:T(8,128)(2,1)S(1)}, bf16[128,512]{1,0:T(8,128)(2,1)S(1)}, u32[]{:S(2)}, u32[]{:S(2)}) collective-permute-start(bf16[128,512]{1,0:T(8,128)(2,1)S(1)} %fusion.82), channel_id=1, source_target_pairs={{0,16},{16,0},{8,24},{24,8},{1,17},{17,1},{9,25},{25,9},{2,18},{18... | collective-permute-start | bytes 393224 | tf_op jit(solution)/shard_map/ppermute | solution.py:18
  549.8 37.0 %collective-permute-start.28 = (bf16[128,512]{1,0:T(8,128)(2,1)S(1)}, bf16[128,512]{1,0:T(8,128)(2,1)S(1)}, u32[]{:S(2)}, u32[]{:S(2)}) collective-permute-start(bf16[128,512]{1,0:T(8,128)(2,1)S(1)} %fusion.109), channel_id=1, source_target_pairs={{0,16},{16,0},{8,24},{24,8},{1,17},{17,1},{9,25},{25,9},{2,18},{18... | collective-permute-start | bytes 393224 | tf_op jit(solution)/shard_map/ppermute | solution.py:18
  583.9 20.7 %collective-permute-start.21 = (f32[128,512]{1,0:T(8,128)S(1)}, f32[128,512]{1,0:T(8,128)S(1)}, u32[]{:S(2)}, u32[]{:S(2)}) collective-permute-start(f32[128,512]{1,0:T(8,128)S(1)} %fusion.117), channel_id=1, source_target_pairs={{0,16},{16,0},{8,24},{24,8},{1,17},{17,1},{9,25},{25,9},{2,18},{18... | collective-permute-start | bytes 786440 | tf_op jit(solution)/shard_map/ppermute | solution.py:18
  (35 other events, 300.3 us)
Sparse Core Ops, SparseCore 0:
  19.6 42.8 all-gather.30
  66.4 38.9 all-gather.18
  107.5 38.9 all-gather.32
  148.5 38.9 all-gather.34
  189.5 38.9 all-gather.20
  230.5 39.0 all-gather.22
  332.5 38.9 all-gather.36
  379.0 38.9 all-gather.24
  420.2 38.9 all-gather.38
  461.1 38.9 all-gather.40
  502.3 38.9 all-gather.26
  543.3 38.9 all-gather.28
where the time goes:
time: 618 us; the launch traced here: 617 us
  waiting for transfers between devices  522 us (84%)
  matrix products  29.3 us (5%)
  starting transfers between devices  23.3 us (4%)
  other arithmetic  20.7 us (3%)
  between operations  14.1 us (2%)
  local copies, waits for them, and re-layouts  7.5 us (1%)
    all_gather x6, waiting for transfers between devices, spread(): return lax.all_gather(cut_cols(values), 'panel', axis=0, tiled=True)  222 us
    ppermute x30, waiting for transfers between devices, partner_2(): return lax.ppermute(block, axis, route)  90.4 us
    all_gather x2, waiting for transfers between devices, star(): lax.all_gather(cut_cols(head_bottom), 'panel', axis=0, tiled=True)  82.1 us
    all_gather x2, waiting for transfers between devices, star(): lax.all_gather(cut_cols(tail_up), 'panel', axis=0, tiled=True)  66.6 us
    all_gather x2, waiting for transfers between devices, star(): lax.all_gather(cut_cols(head_down), 'panel', axis=0, tiled=True)  61 us
    dot_general x28, matrix products, multiply(): jnp.dot(to_half(left), right, preferred_element_type=jnp.float32)  27 us
    ppermute x30, starting transfers between devices, partner_2(): return lax.ppermute(block, axis, route)  22.7 us
  transfers between devices with their start and end apart: 42, of which 28 were waited for; matrix products, arithmetic and copies ran while one was open for 5% of the time, Pallas kernels for 0%

commit v1 on v0

--- a/solution.py
+++ b/solution.py
@@ -23,6 +23,32 @@
 
 
 def star(head, tail, tree_level, row_start):
+
+    def samples_carry(my_tile, which_axis, ndim_at):
+        everything = lax.axis_size(which_axis)
+        left_arr = lax.axis_index(which_axis)
+        y, raw_out, p_next = (everything, left_arr, my_tile.shape[ndim_at])
+        vals = [u * y if j == ndim_at else u for j, u in enumerate(my_tile.shape)]
+        tmp = lax.dynamic_update_slice_in_dim(
+            jnp.zeros(vals, my_tile.dtype), my_tile, raw_out * p_next, axis=ndim_at
+        )
+        arr_out = all_values = my_tile
+        for dev in range(1, y // 2 + 1):
+            arr_out = lax.ppermute(
+                arr_out, which_axis, list(map(lambda j: (j, (j + 1) % y), range(y)))
+            )
+            tmp = lax.dynamic_update_slice_in_dim(
+                tmp, arr_out, (raw_out - dev) % y * p_next, axis=ndim_at
+            )
+            if 2 * dev < y:
+                all_values = lax.ppermute(
+                    all_values, which_axis, list(map(lambda j: (j, (j - 1) % y), range(y)))
+                )
+                tmp = lax.dynamic_update_slice_in_dim(
+                    tmp, all_values, (raw_out + dev) % y * p_next, axis=ndim_at
+                )
+        return tmp
+
     head_top, head_up, head_down, head_bottom = (head[0], head[1], head[2], head[3])
     tail_top, tail_up, tail_down, tail_bottom = (tail[0], tail[1], tail[2], tail[3])
     local_rows = head.shape[1]
@@ -33,7 +59,7 @@
         return lax.dynamic_slice_in_dim(to_half(values), col_start, M // 2, 1)
 
     right_bottom, right_up, right_down = (
-        lax.all_gather(cut_cols(head_bottom), "panel", axis=0, tiled=True),
+        samples_carry(cut_cols(head_bottom), "panel", 0),
         lax.all_gather(cut_cols(tail_up), "panel", axis=0, tiled=True),
         lax.all_gather(cut_cols(head_down), "panel", axis=0, tiled=True),
     )

time: 618 us -> 595 us (0.963)
  waiting for transfers between devices: 522 us -> 473 us
  starting transfers between devices: 23.3 us -> 53.5 us
    all_gather x2 -> x0, waiting for transfers between devices: 82.1 us -> none  [star(): lax.all_gather(cut_cols(head_bottom), 'panel', axis=0, tiled=True)]
    ppermute x0 -> x14, waiting for transfers between devices: none -> 35.1 us  [the longest x8 34.8 us: samples_carry(): lax.ppermute(arr_out, which_axis, list(map(lambda j: (j, (j + 1) % y), ra...]
    ppermute x0 -> x14, starting transfers between devices: none -> 30.2 us  [the longest x6 23.4 us: samples_carry(): lax.ppermute(all_values, which_axis, list(map(lambda j: (j, (j - 1) % y),...]
  transfers between devices with their start and end apart: 42 -> 54, of which waited for: 28 -> 37; matrix products, arithmetic and copies ran while one was open for 5% -> 6% of each run, Pallas kernels for 0% -> 0%
where the time goes in v1:
time: 595 us
  waiting for transfers between devices  473 us (79%)
  starting transfers between devices  53.5 us (9%)
  matrix products  27.4 us (5%)
  other arithmetic  21 us (4%)
  between operations  14.2 us (2%)
    all_gather x6, waiting for transfers between devices, spread(): return lax.all_gather(cut_cols(values), 'panel', axis=0, tiled=True)  218 us
    ppermute x30, waiting for transfers between devices, partner_2(): return lax.ppermute(block, axis, route)  94.9 us
    all_gather x2, waiting for transfers between devices, star(): lax.all_gather(cut_cols(tail_up), 'panel', axis=0, tiled=True)  64.1 us
    all_gather x2, waiting for transfers between devices, star(): lax.all_gather(cut_cols(head_down), 'panel', axis=0, tiled=True)  61.1 us
    ppermute x8, waiting for transfers between devices, samples_carry(): lax.ppermute(arr_out, which_axis, list(map(lambda j: (j, (j + 1) % y), ra...  34.8 us
    dot_general x28, matrix products, multiply(): jnp.dot(to_half(left), right, preferred_element_type=jnp.float32)  25.1 us
    ppermute x6, starting transfers between devices, samples_carry(): lax.ppermute(all_values, which_axis, list(map(lambda j: (j, (j - 1) % y),...  23.4 us
    ppermute x30, starting transfers between devices, partner_2(): return lax.ppermute(block, axis, route)  22.8 us
  transfers between devices with their start and end apart: 54, of which 37 were waited for; matrix products, arithmetic and copies ran while one was open for 6% of the time, Pallas kernels for 0%

profile of v1, /device:TPU:0, one launch (start us, length us, event | category | flops | bytes accessed | tf_op | source)
XLA Modules:
  0.0 594.5 jit_solution(7306875062331463406)
XLA Ops:
  9.4 3.9 collective-permute-done
  13.3 4.4 fusion.127
  24.6 3.9 collective-permute-done.1
  37.8 4.0 collective-permute-start.6
  44.7 8.8 %collective-permute-done.7 = bf16[128,512]{1,0:T(8,128)(2,1)S(1)} collective-permute-done((bf16[128,512]{1,0:T(8,128)(2,1)S(1)}, bf16[128,512]{1,0:T(8,128)(2,1)S(1)}, u32[]{:S(2)}, u32[]{:S(2)}) %collective-permute-start.7) | collective-permute-done | bytes 131104 | tf_op jit(solution)/shard_map/ppermute | solution.py:37
  57.6 37.6 %all-gather.15.cloned.1.call-done = bf16[1024,512]{1,0:T(8,128)(2,1)} async-done(((bf16[128,512]{1,0:T(8,128)(2,1)}), bf16[1024,512]{1,0:T(8,128)(2,1)}) %all-gather.15.cloned.1.call-update) | async-done | bytes 1048592 | tf_op jit(solution)/shard_map/all_gather | solution.py:68
  101.5 34.9 %all-gather.27.cloned.1.call-done = bf16[1,1024,512]{2,1,0:T(8,128)(2,1)} async-done(((bf16[1,128,512]{2,1,0:T(8,128)(2,1)}), bf16[1,1024,512]{2,1,0:T(8,128)(2,1)}) %all-gather.27.cloned.1.call-update) | async-done | bytes 1048592 | tf_op jit(solution)/shard_map/all_gather | solution.py:64
  141.9 35.7 %all-gather.29.cloned.1.call-done = bf16[1,1024,512]{2,1,0:T(8,128)(2,1)} async-done(((bf16[1,128,512]{2,1,0:T(8,128)(2,1)}), bf16[1,1024,512]{2,1,0:T(8,128)(2,1)}) %all-gather.29.cloned.1.call-update) | async-done | bytes 1048592 | tf_op jit(solution)/shard_map/all_gather | solution.py:63
  180.7 37.9 %all-gather.17.cloned.1.call-done = bf16[1024,512]{1,0:T(8,128)(2,1)} async-done(((bf16[128,512]{1,0:T(8,128)(2,1)}), bf16[1024,512]{1,0:T(8,128)(2,1)}) %all-gather.17.cloned.1.call-update) | async-done | bytes 1048592 | tf_op jit(solution)/shard_map/all_gather | solution.py:68
  222.6 37.0 %all-gather.19.cloned.1.call-done = bf16[1024,512]{1,0:T(8,128)(2,1)} async-done(((bf16[128,512]{1,0:T(8,128)(2,1)}), bf16[1024,512]{1,0:T(8,128)(2,1)}) %all-gather.19.cloned.1.call-update) | async-done | bytes 1048592 | tf_op jit(solution)/shard_map/all_gather | solution.py:68
  269.9 46.5 %collective-permute-done.22 = f32[4,128,1024]{2,1,0:T(8,128)} collective-permute-done((f32[4,128,1024]{2,1,0:T(8,128)}, f32[4,128,1024]{2,1,0:T(8,128)}, u32[]{:S(2)}, u32[]{:S(2)}) %collective-permute-start.22) | collective-permute-done | bytes 2097184 | tf_op jit(solution)/shard_map/ppermute | solution.py:18
  316.4 4.4 fusion.125
  321.6 4.1 collective-permute-start.24
  329.4 4.1 collective-permute-start.26
  336.5 4.8 collective-permute-start.28
  344.2 7.6 %collective-permute-done.29 = bf16[128,512]{1,0:T(8,128)(2,1)S(1)} collective-permute-done((bf16[128,512]{1,0:T(8,128)(2,1)S(1)}, bf16[128,512]{1,0:T(8,128)(2,1)S(1)}, u32[]{:S(2)}, u32[]{:S(2)}) %collective-permute-start.29) | collective-permute-done | bytes 131104 | tf_op jit(solution)/shard_map/ppermute | solution.py:37
  359.5 36.1 %all-gather.21.cloned.1.call-done = bf16[1024,512]{1,0:T(8,128)(2,1)} async-done(((bf16[128,512]{1,0:T(8,128)(2,1)}), bf16[1024,512]{1,0:T(8,128)(2,1)}) %all-gather.21.cloned.1.call-update) | async-done | bytes 1048592 | tf_op jit(solution)/shard_map/all_gather | solution.py:68
  404.7 4.7 collective-permute-done.32
  410.5 26.2 %all-gather.31.cloned.1.call-done = bf16[1,1024,512]{2,1,0:T(8,128)(2,1)} async-done(((bf16[1,128,512]{2,1,0:T(8,128)(2,1)}), bf16[1,1024,512]{2,1,0:T(8,128)(2,1)}) %all-gather.31.cloned.1.call-update) | async-done | bytes 1048592 | tf_op jit(solution)/shard_map/all_gather | solution.py:64
  449.4 28.4 %all-gather.33.cloned.1.call-done = bf16[1,1024,512]{2,1,0:T(8,128)(2,1)} async-done(((bf16[1,128,512]{2,1,0:T(8,128)(2,1)}), bf16[1,1024,512]{2,1,0:T(8,128)(2,1)}) %all-gather.33.cloned.1.call-update) | async-done | bytes 1048592 | tf_op jit(solution)/shard_map/all_gather | solution.py:63
  481.9 37.1 %all-gather.23.cloned.1.call-done = bf16[1024,512]{1,0:T(8,128)(2,1)} async-done(((bf16[128,512]{1,0:T(8,128)(2,1)}), bf16[1024,512]{1,0:T(8,128)(2,1)}) %all-gather.23.cloned.1.call-update) | async-done | bytes 1048592 | tf_op jit(solution)/shard_map/all_gather | solution.py:68
  528.0 32.0 %all-gather.25.cloned.1.call-done = bf16[1024,512]{1,0:T(8,128)(2,1)} async-done(((bf16[128,512]{1,0:T(8,128)(2,1)}), bf16[1024,512]{1,0:T(8,128)(2,1)}) %all-gather.25.cloned.1.call-update) | async-done | bytes 1048592 | tf_op jit(solution)/shard_map/all_gather | solution.py:68
  566.3 10.2 %collective-permute-done.36 = f32[128,512]{1,0:T(8,128)S(1)} collective-permute-done((f32[128,512]{1,0:T(8,128)S(1)}, f32[128,512]{1,0:T(8,128)S(1)}, u32[]{:S(2)}, u32[]{:S(2)}) %collective-permute-start.36) | collective-permute-done | bytes 262176 | tf_op jit(solution)/shard_map/ppermute | solution.py:18
  578.2 3.9 collective-permute-done.35
  (206 shorter events, 122.1 us)
Async XLA Ops:
  6.5 88.7 %all-gather.15.cloned.1.call-start = ((), (), s32[]{:S(2)}) async-start(), calls=%async_computation | async-start | bytes 1179648 | tf_op jit(solution)/shard_map/all_gather | solution.py:68
  18.7 9.8 %collective-permute-start.1 = (bf16[128,512]{1,0:T(8,128)(2,1)S(1)}, bf16[128,512]{1,0:T(8,128)(2,1)S(1)}, u32[]{:S(2)}, u32[]{:S(2)}) collective-permute-start(bf16[128,512]{1,0:T(8,128)(2,1)S(1)} %get-tuple-element.12), channel_id=1, source_target_pairs={{0,1},{1,2},{2,3},{3,4},{4,5},{5,6},{6,7},{7,0},{8,9},{9,10},{10,1... | collective-permute-start | bytes 393224 | tf_op jit(solution)/shard_map/ppermute | solution.py:37
  44.7 8.8 %collective-permute-start.7 = (bf16[128,512]{1,0:T(8,128)(2,1)S(1)}, bf16[128,512]{1,0:T(8,128)(2,1)S(1)}, u32[]{:S(2)}, u32[]{:S(2)}) collective-permute-start(bf16[128,512]{1,0:T(8,128)(2,1)S(1)} %collective-permute-done.5), channel_id=1, source_target_pairs={{0,1},{1,2},{2,3},{3,4},{4,5},{5,6},{6,7},{7,0},{8,9},{9,10},{10,1... | collective-permute-start | bytes 393224 | tf_op jit(solution)/shard_map/ppermute | solution.py:37
  56.0 80.3 %all-gather.27.cloned.1.call-start = ((), (), s32[]{:S(2)}) async-start(), calls=%async_computation.6 | async-start | bytes 1179648 | tf_op jit(solution)/shard_map/all_gather | solution.py:64
  56.8 120.8 %all-gather.29.cloned.1.call-start = ((), (), s32[]{:S(2)}) async-start(), calls=%async_computation.7 | async-start | bytes 1179648 | tf_op jit(solution)/shard_map/all_gather | solution.py:63
  57.6 161.0 %all-gather.17.cloned.1.call-start = ((), (), s32[]{:S(2)}) async-start(), calls=%async_computation.1 | async-start | bytes 1179648 | tf_op jit(solution)/shard_map/all_gather | solution.py:68
  101.4 158.2 %all-gather.19.cloned.1.call-start = ((), (), s32[]{:S(2)}) async-start(), calls=%async_computation.2 | async-start | bytes 1179648 | tf_op jit(solution)/shard_map/all_gather | solution.py:68
  140.1 255.5 %all-gather.21.cloned.1.call-start = ((), (), s32[]{:S(2)}) async-start(), calls=%async_computation.3 | async-start | bytes 1179648 | tf_op jit(solution)/shard_map/all_gather | solution.py:68
  179.8 85.5 %collective-permute-start.19 = (f32[128,512]{1,0:T(8,128)}, f32[128,512]{1,0:T(8,128)}, u32[]{:S(2)}, u32[]{:S(2)}) collective-permute-start(f32[128,512]{1,0:T(8,128)} %fusion.24), channel_id=1, source_target_pairs={{0,8},{8,0},{16,24},{24,16},{1,9},{9,1},{17,25},{25,17},{2,10},{10... | collective-permute-start | bytes 786440 | tf_op jit(solution)/shard_map/ppermute | solution.py:18
  180.1 83.7 %collective-permute-start.15 = (f32[128,512]{1,0:T(8,128)S(1)}, f32[128,512]{1,0:T(8,128)S(1)}, u32[]{:S(2)}, u32[]{:S(2)}) collective-permute-start(f32[128,512]{1,0:T(8,128)S(1)} %fusion.28), channel_id=1, source_target_pairs={{0,8},{8,0},{16,24},{24,16},{1,9},{9,1},{17,25},{25,17},{2,10},{10... | collective-permute-start | bytes 786440 | tf_op jit(solution)/shard_map/ppermute | solution.py:18
  221.6 39.7 %collective-permute-start.11 = (bf16[128,512]{1,0:T(8,128)(2,1)S(1)}, bf16[128,512]{1,0:T(8,128)(2,1)S(1)}, u32[]{:S(2)}, u32[]{:S(2)}) collective-permute-start(bf16[128,512]{1,0:T(8,128)(2,1)S(1)} %fusion.75), channel_id=1, source_target_pairs={{0,8},{8,0},{16,24},{24,16},{1,9},{9,1},{17,25},{25,17},{2,10},{10... | collective-permute-start | bytes 393224 | tf_op jit(solution)/shard_map/ppermute | solution.py:18
  222.5 40.0 %collective-permute-start.20 = (bf16[128,512]{1,0:T(8,128)(2,1)S(1)}, bf16[128,512]{1,0:T(8,128)(2,1)S(1)}, u32[]{:S(2)}, u32[]{:S(2)}) collective-permute-start(bf16[128,512]{1,0:T(8,128)(2,1)S(1)} %fusion.115), channel_id=1, source_target_pairs={{0,8},{8,0},{16,24},{24,16},{1,9},{9,1},{17,25},{25,17},{2,10},{10... | collective-permute-start | bytes 393224 | tf_op jit(solution)/shard_map/ppermute | solution.py:18
  268.4 48.0 %collective-permute-start.22 = (f32[4,128,1024]{2,1,0:T(8,128)}, f32[4,128,1024]{2,1,0:T(8,128)}, u32[]{:S(2)}, u32[]{:S(2)}) collective-permute-start(f32[4,128,1024]{2,1,0:T(8,128)} %pad_maximum_fusion), channel_id=1, source_target_pairs={{0,16},{16,0},{8,24},{24,8},{1,17},{17,1},{9,25},{25,9},{2,18},{18... | collective-permute-start | bytes 6291464 | tf_op jit(solution)/shard_map/ppermute | solution.py:18
  357.9 78.8 %all-gather.31.cloned.1.call-start = ((), (), s32[]{:S(2)}) async-start(), calls=%async_computation.8 | async-start | bytes 1179648 | tf_op jit(solution)/shard_map/all_gather | solution.py:64
  358.7 119.2 %all-gather.33.cloned.1.call-start = ((), (), s32[]{:S(2)}) async-start(), calls=%async_computation.9 | async-start | bytes 1179648 | tf_op jit(solution)/shard_map/all_gather | solution.py:63
  359.4 159.6 %all-gather.23.cloned.1.call-start = ((), (), s32[]{:S(2)}) async-start(), calls=%async_computation.4 | async-start | bytes 1179648 | tf_op jit(solution)/shard_map/all_gather | solution.py:68
  410.3 149.7 %all-gather.25.cloned.1.call-start = ((), (), s32[]{:S(2)}) async-start(), calls=%async_computation.5 | async-start | bytes 1179648 | tf_op jit(solution)/shard_map/all_gather | solution.py:68
  479.4 103.9 %collective-permute-start.41 = (f32[128,512]{1,0:T(8,128)S(1)}, f32[128,512]{1,0:T(8,128)S(1)}, u32[]{:S(2)}, u32[]{:S(2)}) collective-permute-start(f32[128,512]{1,0:T(8,128)S(1)} %fusion.14), channel_id=1, source_target_pairs={{0,16},{16,0},{8,24},{24,8},{1,17},{17,1},{9,25},{25,9},{2,18},{18... | collective-permute-start | bytes 786440 | tf_op jit(solution)/shard_map/ppermute | solution.py:18
  481.3 96.8 %collective-permute-start.37 = (f32[128,512]{1,0:T(8,128)S(1)}, f32[128,512]{1,0:T(8,128)S(1)}, u32[]{:S(2)}, u32[]{:S(2)}) collective-permute-start(f32[128,512]{1,0:T(8,128)S(1)} %fusion.18), channel_id=1, source_target_pairs={{0,16},{16,0},{8,24},{24,8},{1,17},{17,1},{9,25},{25,9},{2,18},{18... | collective-permute-start | bytes 786440 | tf_op jit(solution)/shard_map/ppermute | solution.py:18
  523.5 39.6 %collective-permute-start.33 = (bf16[128,512]{1,0:T(8,128)(2,1)S(1)}, bf16[128,512]{1,0:T(8,128)(2,1)S(1)}, u32[]{:S(2)}, u32[]{:S(2)}) collective-permute-start(bf16[128,512]{1,0:T(8,128)(2,1)S(1)} %fusion.74), channel_id=1, source_target_pairs={{0,16},{16,0},{8,24},{24,8},{1,17},{17,1},{9,25},{25,9},{2,18},{18... | collective-permute-start | bytes 393224 | tf_op jit(solution)/shard_map/ppermute | solution.py:18
  527.5 37.0 %collective-permute-start.42 = (bf16[128,512]{1,0:T(8,128)(2,1)S(1)}, bf16[128,512]{1,0:T(8,128)(2,1)S(1)}, u32[]{:S(2)}, u32[]{:S(2)}) collective-permute-start(bf16[128,512]{1,0:T(8,128)(2,1)S(1)} %fusion.105), channel_id=1, source_target_pairs={{0,16},{16,0},{8,24},{24,8},{1,17},{17,1},{9,25},{25,9},{2,18},{18... | collective-permute-start | bytes 393224 | tf_op jit(solution)/shard_map/ppermute | solution.py:18
  561.7 16.4 %collective-permute-start.40 = (f32[128,512]{1,0:T(8,128)S(1)}, f32[128,512]{1,0:T(8,128)S(1)}, u32[]{:S(2)}, u32[]{:S(2)}) collective-permute-start(f32[128,512]{1,0:T(8,128)S(1)} %fusion.107), channel_id=1, source_target_pairs={{0,16},{16,0},{8,24},{24,8},{1,17},{17,1},{9,25},{25,9},{2,18},{18... | collective-permute-start | bytes 786440 | tf_op jit(solution)/shard_map/ppermute | solution.py:18
  563.5 13.0 %collective-permute-start.36 = (f32[128,512]{1,0:T(8,128)S(1)}, f32[128,512]{1,0:T(8,128)S(1)}, u32[]{:S(2)}, u32[]{:S(2)}) collective-permute-start(f32[128,512]{1,0:T(8,128)S(1)} %fusion.16), channel_id=1, source_target_pairs={{0,16},{16,0},{8,24},{24,8},{1,17},{17,1},{9,25},{25,9},{2,18},{18... | collective-permute-start | bytes 786440 | tf_op jit(solution)/shard_map/ppermute | solution.py:18
  564.5 17.6 %collective-permute-start.35 = (f32[128,512]{1,0:T(8,128)S(1)}, f32[128,512]{1,0:T(8,128)S(1)}, u32[]{:S(2)}, u32[]{:S(2)}) collective-permute-start(f32[128,512]{1,0:T(8,128)S(1)} %fusion.113), channel_id=1, source_target_pairs={{0,16},{16,0},{8,24},{24,8},{1,17},{17,1},{9,25},{25,9},{2,18},{18... | collective-permute-start | bytes 786440 | tf_op jit(solution)/shard_map/ppermute | solution.py:18
  (45 other events, 386.5 us)
Sparse Core Ops, SparseCore 0:
  56.2 38.9 all-gather.14
  97.3 38.9 all-gather.26
  138.5 39.0 all-gather.28
  179.5 38.9 all-gather.16
  220.5 39.0 all-gather.18
  358.0 37.4 all-gather.20
  397.7 38.9 all-gather.30
  438.9 38.9 all-gather.32
  480.0 38.9 all-gather.22
  521.0 38.9 all-gather.24
